TPU v7x, 32 devices: a whole 2x2x4 slice. The times are simulated.
32 devices in a mesh: fsdp: 32 (over z, y, x, core).
Axes of the slice: x: 2, y: 2, z: 4, core: 2. Of those that a mesh axis runs over, the one named last changes fastest.
Arguments:
- inputs: bfloat16 [32, 128, 768], P('fsdp'), may hold values from -6 to 6
- encoded: bfloat16 [32, 64, 768], P('fsdp')
- lengths: int32 [32], P('fsdp'), may hold values from 32 to 128, as said below
- bucket_ids: int32 [128], replicated, may hold values from 0 to 31, as said below
- qkv_weights: bfloat16 [768, 6, 768], P('fsdp')
- out_weights: bfloat16 [768, 2, 768], P('fsdp'), may hold values from -1.75 to 1.75
- ff_in: bfloat16 [768, 2, 2048], P('fsdp'), may hold values from -0.21875 to 0.21875
- ff_out: bfloat16 [2048, 768], P('fsdp'), may hold values from -0.125 to 0.125
- gains: bfloat16 [3, 768], P(None, 'fsdp'), may hold values from 0.5 to 1.5
- bias_table: float32 [32, 12], replicated
- cotangent: bfloat16 [32, 128, 768], P('fsdp'), may hold values from -6 to 6
Outputs:
- outputs: bfloat16 [32, 128, 768], P('fsdp')
- input_grad: bfloat16 [32, 128, 768], P('fsdp')
- encoded_grad: bfloat16 [32, 64, 768], P('fsdp')
- qkv_grad: float32 [768, 6, 768], P('fsdp')
- out_grad: float32 [768, 2, 768], P('fsdp')
- ffin_grad: float32 [768, 2, 2048], P('fsdp')
- ffout_grad: float32 [2048, 768], P('fsdp')
- gain_grad: float32 [3, 768], P(None, 'fsdp')
- table_grad: float32 [32, 12], replicated
Inputs may be any that keep to these rules, and one draw needn't show every extreme that they name: `lengths`: some sequence uses all 128 slots. `bucket_ids`: non-decreasing in the distance; distance 0 has bucket 0 and distance 128 - 1 bucket 32 - 1.
All inputs are finite; a program needn't handle non-finite values.
Results may differ from a plain program's by a relative error of at most 0.02.
Values may be sent and summed in bfloat16 or wider, within the bound.
A program may use at most 192 MiB of HBM per device.

v0:
```python
import jax
import jax.numpy as jnp
from jax import lax
from jax.sharding import PartitionSpec as P

HEAD = 64
EPS = 1e-06


def prod(form, left, right):
    return jnp.einsum(form, left, right, preferred_element_type=jnp.float32)


def gelu_tanh(value):
    return (
        0.5
        * value
        * (1.0 + jnp.tanh(0.7978845608028654 * (value + 0.044715 * value * value * value)))
    )


def rms_fwd(value, gain):
    recip = lax.rsqrt(jnp.mean(value * value, axis=-1, keepdims=True) + EPS)
    normed = value * recip
    return ((normed * gain).astype(jnp.bfloat16), normed, recip)


def rms_bwd(grad, normed, recip, gain):
    scaled = grad * gain
    gain_grad = jnp.sum(grad * normed, axis=0)
    back = recip * (scaled - normed * jnp.mean(scaled * normed, axis=-1, keepdims=True))
    return (back, gain_grad)


def toeplitz_bias(bucket_ids, table, positions):
    onehot = (bucket_ids[:, None] == jnp.arange(table.shape[0], dtype=jnp.int32)[None, :]).astype(
        jnp.float32
    )
    by_dist = jnp.transpose(jnp.dot(onehot, table, precision=lax.Precision.HIGHEST), (1, 0))
    head_count = by_dist.shape[0]
    nearest = jnp.broadcast_to(by_dist[:, 0:1], (head_count, positions))
    cyclic = jnp.concatenate(
        [nearest, jnp.zeros((head_count, 1), jnp.float32), by_dist[:, :0:-1]], axis=1
    )
    tiled = jnp.broadcast_to(cyclic[:, None, :], (head_count, positions, 2 * positions))
    tiled = tiled.reshape(head_count, 2 * positions * positions)
    skewed = tiled[:, : positions * (2 * positions - 1)].reshape(
        head_count, positions, 2 * positions - 1
    )
    return (skewed[:, :, :positions], onehot)


def diagonal_sums(d_score, onehot):
    head_count, positions = (d_score.shape[0], d_score.shape[1])
    padded = jnp.pad(d_score, ((0, 0), (0, 0), (0, positions - 1)))
    padded = padded.reshape(head_count, positions * (2 * positions - 1))
    padded = jnp.pad(padded, ((0, 0), (0, positions))).reshape(head_count, positions, 2 * positions)
    column = jnp.sum(padded, axis=1)
    by_dist = jnp.concatenate(
        [jnp.sum(column[:, :positions], axis=1, keepdims=True), column[:, :positions:-1]], axis=1
    )
    return jnp.dot(
        jnp.transpose(onehot, (1, 0)),
        jnp.transpose(by_dist, (1, 0)),
        precision=lax.Precision.HIGHEST,
    )


def scores_of(query, keys, bias, mask):
    rows = query.shape[0]
    q3 = query.reshape(rows, -1, HEAD)
    k3 = keys.reshape(keys.shape[0], -1, HEAD)
    scores = prod("qhd,khd->hqk", q3, k3)
    if bias is not None:
        scores = scores + bias
    if mask is not None:
        scores = jnp.where(mask[None], scores, -1e30)
    return scores


def attend(query, keys, values, bias, mask, shifted):
    rows = query.shape[0]
    scores = scores_of(query, keys, bias, mask)
    if shifted:
        top = jnp.max(scores, axis=-1, keepdims=True)
        lse = top + jnp.log(jnp.sum(jnp.exp(scores - top), axis=-1, keepdims=True))
    else:
        lse = jnp.log(jnp.sum(jnp.exp(scores), axis=-1, keepdims=True))
    prob = jnp.exp(scores - lse).astype(jnp.bfloat16)
    v3 = values.reshape(values.shape[0], -1, HEAD)
    out = prod("hqk,khd->qhd", prob, v3).reshape(rows, -1).astype(jnp.bfloat16)
    return (out, lse)


def attend_back(query, keys, values, out, lse, grad_out, bias, mask):
    rows = query.shape[0]
    scores = scores_of(query, keys, bias, mask)
    prob = jnp.exp(scores - lse)
    prob_b = prob.astype(jnp.bfloat16)
    q3 = query.reshape(rows, -1, HEAD)
    k3 = keys.reshape(keys.shape[0], -1, HEAD)
    v3 = values.reshape(values.shape[0], -1, HEAD)
    grad3 = grad_out.reshape(rows, -1, HEAD)
    grad_b = grad3.astype(jnp.bfloat16)
    out3 = out.reshape(rows, -1, HEAD).astype(jnp.float32)
    d_val = prod("hqk,qhd->khd", prob_b, grad_b)
    d_prob = prod("qhd,khd->hqk", grad_b, v3)
    delta = jnp.transpose(jnp.sum(grad3 * out3, axis=2), (1, 0))
    d_score = prob * (d_prob - delta[:, :, None])
    d_score_b = d_score.astype(jnp.bfloat16)
    d_query = prod("hqk,khd->qhd", d_score_b, k3)
    d_key = prod("hqk,qhd->khd", d_score_b, q3)
    shape_q = (rows, -1)
    shape_k = (keys.shape[0], -1)
    return (
        d_query.reshape(shape_q).astype(jnp.bfloat16),
        d_key.reshape(shape_k).astype(jnp.bfloat16),
        d_val.reshape(shape_k).astype(jnp.bfloat16),
        d_score,
    )


def forward(rows, enc, length, bucket_ids, weights, table):
    qkv_w, out_w, ff_in, ff_out, gains = weights
    positions = rows.shape[0]
    gain_f = gains.astype(jnp.float32)
    start = rows.astype(jnp.float32)
    h1, n1, r1 = rms_fwd(start, gain_f[0])
    qkv = prod("ld,cde->cle", h1, qkv_w[0:3]).astype(jnp.bfloat16)
    row_ids = lax.broadcasted_iota(jnp.int32, (positions, positions), 0)
    col_ids = lax.broadcasted_iota(jnp.int32, (positions, positions), 1)
    mask = (col_ids <= row_ids) & (col_ids < length)
    bias, onehot = toeplitz_bias(bucket_ids, table, positions)
    a1, lse1 = attend(qkv[0], qkv[1], qkv[2], bias, mask, True)
    x1 = start + prod("le,ed->ld", a1, out_w[0])
    h2, n2, r2 = rms_fwd(x1, gain_f[1])
    qc = prod("ld,de->le", h2, qkv_w[3]).astype(jnp.bfloat16)
    kvc = prod("ld,cde->cle", enc, qkv_w[4:6]).astype(jnp.bfloat16)
    ac, lse2 = attend(qc, kvc[0], kvc[1], None, None, False)
    x2 = x1 + prod("le,ed->ld", ac, out_w[1])
    h3, n3, r3 = rms_fwd(x2, gain_f[2])
    gate_up = prod("ld,cdf->clf", h3, ff_in)
    hidden = (gelu_tanh(gate_up[0]) * gate_up[1]).astype(jnp.bfloat16)
    result = x2 + prod("lf,fd->ld", hidden, ff_out)
    saved = (
        h1,
        n1,
        r1,
        qkv,
        bias,
        mask,
        a1,
        lse1,
        h2,
        n2,
        r2,
        qc,
        kvc,
        ac,
        lse2,
        h3,
        n3,
        r3,
        gate_up,
        hidden,
        onehot,
    )
    return (result.astype(jnp.bfloat16), saved)


def ff_back(saved, weights, cot):
    qkv_w, out_w, ff_in, ff_out, gains = weights
    gain_f = gains.astype(jnp.float32)
    h3, n3, r3, gate_up, hidden = (saved[15], saved[16], saved[17], saved[18], saved[19])
    d_ffout = prod("lf,ld->fd", hidden, cot)
    d_hidden = prod("ld,fd->lf", cot, ff_out)
    gelu_val, gelu_pull = jax.vjp(gelu_tanh, gate_up[0])
    d_gate = gelu_pull(d_hidden * gate_up[1])[0]
    d_up = d_hidden * gelu_val
    d_gate_up = jnp.stack([d_gate, d_up]).astype(jnp.bfloat16)
    d_ffin = prod("ld,clf->cdf", h3, d_gate_up)
    d_h3 = prod("clf,cdf->ld", d_gate_up, ff_in)
    back3, gain3 = rms_bwd(d_h3, n3, r3, gain_f[2])
    return (cot.astype(jnp.float32) + back3, d_ffin, d_ffout, gain3)


def cross_back(saved, weights, enc, dx2):
    qkv_w, out_w, ff_in, ff_out, gains = weights
    gain_f = gains.astype(jnp.float32)
    h2, n2, r2, qc, kvc, ac, lse2 = (
        saved[8],
        saved[9],
        saved[10],
        saved[11],
        saved[12],
        saved[13],
        saved[14],
    )
    dx2_b = dx2.astype(jnp.bfloat16)
    d_outc = prod("le,ld->ed", ac, dx2_b)
    d_ac = prod("ld,ed->le", dx2_b, out_w[1])
    d_qc, d_kc, d_vc, unused = attend_back(qc, kvc[0], kvc[1], ac, lse2, d_ac, None, None)
    g_qc = prod("ld,le->de", h2, d_qc)
    d_kvc = jnp.stack([d_kc, d_vc])
    g_kvc = prod("ld,cle->cde", enc, d_kvc)
    enc_grad = prod("cle,cde->ld", d_kvc, qkv_w[4:6]).astype(jnp.bfloat16)
    d_h2 = prod("le,de->ld", d_qc, qkv_w[3])
    back2, gain2 = rms_bwd(d_h2, n2, r2, gain_f[1])
    return (dx2 + back2, g_qc, g_kvc, d_outc, gain2, enc_grad)


def self_back(saved, weights, dx1):
    qkv_w, out_w, ff_in, ff_out, gains = weights
    gain_f = gains.astype(jnp.float32)
    h1, n1, r1, qkv, bias, mask, a1, lse1 = saved[0:8]
    onehot = saved[20]
    dx1_b = dx1.astype(jnp.bfloat16)
    d_outs = prod("le,ld->ed", a1, dx1_b)
    d_a1 = prod("ld,ed->le", dx1_b, out_w[0])
    d_q, d_k, d_v, d_score = attend_back(qkv[0], qkv[1], qkv[2], a1, lse1, d_a1, bias, mask)
    d_qkv = jnp.stack([d_q, d_k, d_v])
    g_qkv = prod("ld,cle->cde", h1, d_qkv)
    d_h1 = prod("cle,cde->ld", d_qkv, qkv_w[0:3])
    back1, gain1 = rms_bwd(d_h1, n1, r1, gain_f[0])
    d_table = diagonal_sums(d_score, onehot)
    return ((dx1 + back1).astype(jnp.bfloat16), g_qkv, d_outs, gain1, d_table)


def to_blocks(array, width):
    blocks = []
    for copy in range(array.shape[0]):
        for start in range(0, array.shape[-1], width):
            block = array[copy, ..., start : start + width]
            short = width - block.shape[-1]
            if short:
                block = jnp.pad(block, ((0, 0),) * (block.ndim - 1) + ((0, short),))
            blocks.append(block)
    return blocks


def from_blocks(blocks, shape, width):
    copies, rows, columns = shape
    each = -(-columns // width)
    planes = []
    for copy in range(copies):
        part = [blocks[copy * each + at] for at in range(each)]
        part[-1] = part[-1][..., : columns - (each - 1) * width]
        planes.append(part[0] if each == 1 else jnp.concatenate(part, axis=-1))
    return planes


def per_device(
    inputs,
    encoded,
    lengths,
    bucket_ids,
    qkv_weights,
    out_weights,
    ff_in,
    ff_out,
    gains,
    bias_table,
    cotangent,
):
    count = lax.axis_size("fsdp")
    shards = (
        jnp.transpose(qkv_weights, (1, 0, 2)),
        jnp.transpose(out_weights, (1, 0, 2)),
        jnp.transpose(ff_in, (1, 0, 2)),
        ff_out[None],
    )
    width = qkv_weights.shape[-1]
    depth = qkv_weights.shape[0]
    tall = ff_out.shape[0]
    blocks = to_blocks(shards[0], width) + to_blocks(shards[1], width) + to_blocks(shards[2], width)
    slots = gains.size
    tail = 8 * -(-slots // (8 * width))
    gain_rows = jnp.pad(gains.reshape(1, slots), ((0, 0), (0, tail * width - slots)))
    packed = jnp.concatenate(blocks + [ff_out, gain_rows.reshape(tail, width)], axis=0)
    whole = lax.all_gather(packed, "fsdp", axis=0, tiled=False)
    cut = len(blocks) * depth
    stacked = whole[:, :cut].reshape(count, len(blocks), depth, width)
    stacked = jnp.transpose(stacked, (1, 0, 2, 3)).reshape(len(blocks), count * depth, width)
    ff_out_all = whole[:, cut : cut + tall].reshape(count * tall, width)
    stacked, ff_out_all = lax.optimization_barrier((stacked, ff_out_all))
    n_qkv, n_out = (qkv_weights.shape[1], out_weights.shape[1])
    ff_all = jnp.stack(from_blocks(stacked[n_qkv + n_out :], shards[2].shape, width))
    main = (stacked[:n_qkv], stacked[n_qkv : n_qkv + n_out], ff_all, ff_out_all[None])
    gain_all = whole[:, -tail:].reshape(count, tail * width)[:, :slots]
    gain_all = gain_all.reshape(count, gains.shape[0], gains.shape[1])
    gain_all = jnp.transpose(gain_all, (1, 0, 2)).reshape(gains.shape[0], -1)
    weights = (main[0], main[1], main[2], main[3][0], gain_all)
    result, saved = forward(inputs[0], encoded[0], lengths[0], bucket_ids, weights, bias_table)
    dx2, g_ffin, g_ffout, gain3 = ff_back(saved, weights, cotangent[0])
    dx1, g_qc, g_kvc, g_outc, gain2, enc_grad = cross_back(saved, weights, encoded[0], dx2)
    dx, g_qkvs, g_outs, gain1, g_table = self_back(saved, weights, dx1)
    wide = [g_qkvs[0], g_qkvs[1], g_qkvs[2], g_qc, g_kvc[0], g_kvc[1], g_outs, g_outc]
    wide += to_blocks(g_ffin, width)
    wide.append(g_ffout)
    g_gain = jnp.stack([gain1, gain2, gain3]).reshape(gains.shape[0], count, -1)
    g_gain = jnp.transpose(g_gain, (1, 0, 2)).reshape(count, slots)
    g_gain = jnp.pad(g_gain, ((0, 0), (0, tail * width - slots))).reshape(count, tail, width)
    parts = [grad.astype(jnp.bfloat16).reshape(count, -1, width) for grad in wide]
    send = jnp.concatenate(parts + [g_gain.astype(jnp.bfloat16)], axis=1)
    send, g_table = lax.optimization_barrier((send, g_table))
    own = lax.psum_scatter(send, "fsdp", scatter_dimension=0, tiled=False).astype(jnp.float32)
    mine = own[:cut].reshape(len(blocks), depth, width)
    s_ffin = jnp.stack(from_blocks(mine[n_qkv + n_out :], shards[2].shape, width))
    s_main = (mine[:n_qkv], mine[n_qkv : n_qkv + n_out], s_ffin, own[cut : cut + tall][None])
    s_gain = own[-tail:].reshape(tail * width)[:slots].reshape(gains.shape)
    s_table = lax.psum(g_table, "fsdp")
    return (
        result[None],
        dx[None],
        enc_grad[None],
        jnp.transpose(s_main[0], (1, 0, 2)),
        jnp.transpose(s_main[1], (1, 0, 2)),
        jnp.transpose(s_main[2], (1, 0, 2)),
        s_main[3][0],
        s_gain,
        s_table,
    )


def solution(mesh):
    placed = (
        P("fsdp", None, None),
        P("fsdp", None, None),
        P("fsdp"),
        P(),
        P("fsdp", None, None),
        P("fsdp", None, None),
        P("fsdp", None, None),
        P("fsdp", None),
        P(None, "fsdp"),
        P(),
        P("fsdp", None, None),
    )
    return jax.shard_map(
        per_device,
        mesh=mesh,
        in_specs=placed,
        out_specs=(
            P("fsdp", None, None),
            P("fsdp", None, None),
            P("fsdp", None, None),
            P("fsdp", None, None),
            P("fsdp", None, None),
            P("fsdp", None, None),
            P("fsdp", None),
            P(None, "fsdp"),
            P(),
        ),
        check_vma=False,
    )
```

profile of v0, /device:TPU:0, one launch (start us, length us, event | category | flops | bytes accessed | tf_op | source)
XLA Modules:
  0.0 536.2 jit_solution(1657681668492004055)
XLA Ops:
  19.7 3.4 reshape.321
  25.4 123.4 %all-gather.3.cloned.1.call-done = bf16[13056,768]{1,0:T(8,128)(2,1)} async-done(((bf16[408,768]{1,0:T(8,128)(2,1)}), bf16[13056,768]{1,0:T(8,128)(2,1)}) %all-gather.3.cloned.1.call-update) | async-done | bytes 20054032 | tf_op jit(solution)/shard_map/all_gather | solution.py:280
  148.8 7.9 %slice.390 = bf16[32,336,768]{2,1,0:T(8,128)(2,1)S(1)} slice(bf16[32,408,768]{2,1,0:T(8,128)(2,1)} %bitcast.363), slice={[0:32], [0:336], [0:768]} | slice | bytes 33030144 | tf_op jit(solution)/shard_map/slice | solution.py:282
  156.8 3.9 slice.391
  161.7 6.6 %copy.95 = bf16[14,32,24,768]{3,2,1,0:T(8,128)(2,1)} copy(bf16[14,32,24,768]{3,2,0,1:T(8,128)(2,1)S(1)} %bitcast.362) | data formatting | bytes 33030144 | tf_op jit(solution)/shard_map/transpose | solution.py:283
  168.3 22.3 %copy.96 = bf16[14,768,768]{1,2,0:T(8,128)(2,1)} copy(bf16[14,768,768]{2,1,0:T(8,128)(2,1)} %bitcast.353) | data formatting | bytes 33030144 | tf_op jit(solution)/shard_map/optimization_barrier | solution.py:285
  190.6 3.2 fusion.154
  194.8 3.2 fusion.12
  200.7 2.2 fusion.35
  209.2 5.2 slice_bitcast_fusion.5
  216.4 3.0 maximum_bitcast_fusion
  226.7 2.6 multiply_reduce_fusion.1
  235.3 4.0 fusion.84
  239.3 2.9 convert_bitcast_fusion.1
  249.0 2.2 fusion.155
  254.6 2.3 copy.150
  256.9 2.5 pad.39.clone
  259.3 3.9 reshape.330
  269.1 3.7 fusion.156
  287.6 2.4 copy.130
  292.0 2.5 constant_dynamic-update-slice_fusion.30
  311.9 38.4 %psum.7 = f32[32,12]{0,1:T(8,128)} all-reduce(f32[32,12]{0,1:T(8,128)S(1)} %fusion.123), channel_id=1, replica_groups=mesh['fsdp'=32] {'fsdp'}, use_global_device_ids=true, to_apply=%region_17.18 | all-reduce | flops 384 | bytes 3072 | tf_op jit(solution)/shard_map/psum | solution.py:311
  350.3 3.5 fusion.45
  357.2 166.7 %reduce-scatter.2.cloned.1.call-done = bf16[1,408,768]{2,1,0:T(8,128)(2,1)} async-done(((bf16[32,408,768]{2,1,0:T(8,128)(2,1)}), bf16[1,408,768]{2,1,0:T(8,128)(2,1)}) %reduce-scatter.2.cloned.1.call-update) | async-done | bytes 626704 | tf_op jit(solution)/shard_map/reduce_scatter | solution.py:306
  (287 shorter events, 98.6 us)
Async XLA Ops:
  7.2 193.5 %copy-start = (bf16[1,64,768]{2,1,0:T(8,128)(2,1)S(1)}, bf16[1,64,768]{2,1,0:T(8,128)(2,1)}, u32[]{:S(2)}) copy-start(bf16[1,64,768]{2,1,0:T(8,128)(2,1)} %param.12) | copy-start | bytes 294916
  7.2 141.7 %all-gather.3.cloned.1.call-start = ((), (), s32[]{:S(2)}) async-start(), calls=%async_computation.2 | async-start | bytes 20680704 | tf_op jit(solution)/shard_map/all_gather | solution.py:280
  16.5 507.4 %reduce-scatter.2.cloned.1.call-start = ((), (), s32[]{:S(2)}) async-start(), calls=%async_computation.1 | async-start | bytes 20680704 | tf_op jit(solution)/shard_map/reduce_scatter | solution.py:306
  19.7 5.5 %copy-start.4 = (bf16[1,128,768]{2,1,0:T(8,128)(2,1)S(1)}, bf16[1,128,768]{2,1,0:T(8,128)(2,1)}, u32[]{:S(2)}) copy-start(bf16[1,128,768]{2,1,0:T(8,128)(2,1)} %param.11) | copy-start | bytes 589828
  198.1 4.8 copy-start.34
  198.1 4.8 copy-start.36
  198.1 4.8 copy-start.38
  198.8 6.2 %copy-start.26 = (bf16[12,64,128]{2,1,0:T(8,128)(2,1)}, bf16[12,64,128]{2,1,0:T(8,128)(2,1)S(1)}, u32[]{:S(2)}) copy-start(bf16[12,64,128]{2,1,0:T(8,128)(2,1)S(1)} %convolution_convert_fusion.12) | copy-start | bytes 589828
  209.1 15.7 %copy-start.19 = (f32[128,768]{1,0:T(8,128)}, f32[128,768]{1,0:T(8,128)S(1)}, u32[]{:S(2)}) copy-start(f32[128,768]{1,0:T(8,128)S(1)} %get-tuple-element.94) | copy-start | bytes 1179652
  229.4 14.5 %copy-start.2 = (f32[128,768]{1,0:T(8,128)}, f32[128,768]{1,0:T(8,128)S(1)}, u32[]{:S(2)}) copy-start(f32[128,768]{1,0:T(8,128)S(1)} %multiply_add_fusion.3) | copy-start | bytes 1179652
  230.0 4.0 copy-start.31
  239.3 4.5 copy-start.28
  239.3 6.0 %copy-start.42 = (bf16[12,64,128]{2,1,0:T(8,128)(2,1)S(1)}, bf16[12,64,128]{2,1,0:T(8,128)(2,1)}, u32[]{:S(2)}) copy-start(bf16[12,64,128]{2,1,0:T(8,128)(2,1)} %copy-done.40) | copy-start | bytes 589828
  242.3 4.6 copy-start.20
  242.3 4.6 copy-start.58
  242.3 4.6 copy-start.60
  269.1 4.8 copy-start.64
  292.0 4.8 copy-start.16
  311.8 38.5 %copy-start.67 = (f32[128]{0:T(128)S(1)}, f32[128]{0:T(128)}, u32[]{:S(2)}) copy-start(f32[128]{0:T(128)} %get-tuple-element.49) | copy-start | bytes 1540
  311.8 38.5 %copy-start.65 = (bf16[1,64,768]{2,1,0:T(8,128)(2,1)S(1)}, bf16[1,64,768]{2,1,0:T(8,128)(2,1)}, u32[]{:S(2)}) copy-start(bf16[1,64,768]{2,1,0:T(8,128)(2,1)} %copy.124) | copy-start | bytes 294916
  311.8 43.9 %copy-start.63 = (f32[2,128,2048]{1,2,0:T(8,128)S(1)}, f32[2,128,2048]{1,2,0:T(8,128)}, u32[]{:S(2)}) copy-start(f32[2,128,2048]{1,2,0:T(8,128)} %copy-done.61) | copy-start | bytes 6291460
  311.9 41.9 %copy-start.3 = (f32[128,768]{1,0:T(8,128)S(1)}, f32[128,768]{1,0:T(8,128)}, u32[]{:S(2)}) copy-start(f32[128,768]{1,0:T(8,128)} %copy-done.2) | copy-start | bytes 1179652
  311.9 43.8 %copy-start.21 = (f32[128,768]{1,0:T(8,128)S(1)}, f32[128,768]{1,0:T(8,128)}, u32[]{:S(2)}) copy-start(f32[128,768]{1,0:T(8,128)} %copy-done.19) | copy-start | bytes 1179652
  350.3 5.4 %copy-start.23 = (bf16[32,64,768]{2,1,0:T(8,128)(2,1)S(1)}, bf16[32,64,768]{2,1,0:T(8,128)(2,1)}, u32[]{:S(2)}) copy-start(bf16[32,64,768]{2,1,0:T(8,128)(2,1)} %slice.391) | copy-start | bytes 9437188
  (46 other events, 112.4 us)
Sparse Core Ops, SparseCore 0:
  16.6 132.1 all-gather.2
  312.0 211.8 reduce-scatter.1
where the time goes:
time: 538 us; the launch traced here: 536 us
  waiting for transfers between devices  290 us (54%)
  local copies, waits for them, and re-layouts  134 us (25%)
  matrix products  47.5 us (9%)
  blocking collectives  38.4 us (7%)
  between operations  15.8 us (3%)
  other arithmetic  10 us (2%)
    reduce_scatter x1, waiting for transfers between devices, per_device(): lax.psum_scatter(send, 'fsdp', scatter_dimension=0, tiled=False)  167 us
    all_gather x1, waiting for transfers between devices, per_device(): whole = lax.all_gather(packed, 'fsdp', axis=0, tiled=False)  123 us
    dot_general x33, matrix products, prod(): return jnp.einsum(form, left, right, preferred_element_type=jnp.float32)  45.6 us
    psum x1, blocking collectives, per_device(): s_table = lax.psum(g_table, 'fsdp')  38.4 us
    unnamed x174, local copies, waits for them, and re-layouts  36.2 us
    optimization_barrier x1, local copies, waits for them, and re-layouts, per_device(): stacked, ff_out_all = lax.optimization_barrier((stacked, ff_out_all))  22.3 us
  transfers between devices with their start and end apart: 2, of which 2 were waited for; matrix products, arithmetic and copies ran while one was open for 3% of the time, Pallas kernels for 0%

commit v1 on v0

--- a/solution.py
+++ b/solution.py
@@ -308,7 +308,9 @@
     s_ffin = jnp.stack(from_blocks(mine[n_qkv + n_out :], shards[2].shape, width))
     s_main = (mine[:n_qkv], mine[n_qkv : n_qkv + n_out], s_ffin, own[cut : cut + tall][None])
     s_gain = own[-tail:].reshape(tail * width)[:slots].reshape(gains.shape)
-    s_table = lax.psum(g_table, "fsdp")
+    s_table = g_table
+    for hop in (1, 2, 4, 8, 16):
+        s_table = s_table + lax.ppermute(s_table, "fsdp", [(dev, dev ^ hop) for dev in range(32)])
     return (
         result[None],
         dx[None],

time: 538 us -> 539 us (level)
  blocking collectives: 38.4 us -> 0 us
  waiting for transfers between devices: 290 us -> 324 us
    psum x1 -> x0, blocking collectives: 38.4 us -> none  [per_device(): s_table = lax.psum(g_table, 'fsdp')]
    reduce_scatter x1, waiting for transfers between devices: 167 us -> 193 us  [per_device(): lax.psum_scatter(send, 'fsdp', scatter_dimension=0, tiled=False)]
    ppermute x0 -> x5, waiting for transfers between devices: none -> 7.24 us  [per_device(): lax.ppermute(s_table, 'fsdp', [(dev, dev ^ hop) for dev in range(32)])]
  transfers between devices with their start and end apart: 2 -> 7, of which waited for: 2 -> 6; matrix products, arithmetic and copies ran while one was open for 3% -> 3% of each run, Pallas kernels for 0% -> 0%
where the time goes in v1:
time: 539 us; the launch traced here: 536 us
  waiting for transfers between devices  324 us (60%)
  local copies, waits for them, and re-layouts  134 us (25%)
  matrix products  49.6 us (9%)
  between operations  15.8 us (3%)
  other arithmetic  9.61 us (2%)
    reduce_scatter x1, waiting for transfers between devices, per_device(): lax.psum_scatter(send, 'fsdp', scatter_dimension=0, tiled=False)  193 us
    all_gather x1, waiting for transfers between devices, per_device(): whole = lax.all_gather(packed, 'fsdp', axis=0, tiled=False)  123 us
    dot_general x33, matrix products, prod(): return jnp.einsum(form, left, right, preferred_element_type=jnp.float32)  47.8 us
    unnamed x174, local copies, waits for them, and re-layouts  36.3 us
    optimization_barrier x1, local copies, waits for them, and re-layouts, per_device(): stacked, ff_out_all = lax.optimization_barrier((stacked, ff_out_all))  22.3 us
  transfers between devices with their start and end apart: 7, of which 6 were waited for; matrix products, arithmetic and copies ran while one was open for 3% of the time, Pallas kernels for 0%

profile of v1, /device:TPU:0, one launch (start us, length us, event | category | flops | bytes accessed | tf_op | source)
XLA Modules:
  0.0 536.3 jit_solution(10097828467222876438)
XLA Ops:
  19.7 3.4 reshape.321
  25.4 123.4 %all-gather.3.cloned.1.call-done = bf16[13056,768]{1,0:T(8,128)(2,1)} async-done(((bf16[408,768]{1,0:T(8,128)(2,1)}), bf16[13056,768]{1,0:T(8,128)(2,1)}) %all-gather.3.cloned.1.call-update) | async-done | bytes 20054032 | tf_op jit(solution)/shard_map/all_gather | solution.py:280
  148.8 7.9 %slice.390 = bf16[32,336,768]{2,1,0:T(8,128)(2,1)S(1)} slice(bf16[32,408,768]{2,1,0:T(8,128)(2,1)} %bitcast.363), slice={[0:32], [0:336], [0:768]} | slice | bytes 33030144 | tf_op jit(solution)/shard_map/slice | solution.py:282
  156.8 3.9 slice.391
  161.7 6.6 %copy.95 = bf16[14,32,24,768]{3,2,1,0:T(8,128)(2,1)} copy(bf16[14,32,24,768]{3,2,0,1:T(8,128)(2,1)S(1)} %bitcast.362) | data formatting | bytes 33030144 | tf_op jit(solution)/shard_map/transpose | solution.py:283
  168.2 22.3 %copy.96 = bf16[14,768,768]{1,2,0:T(8,128)(2,1)} copy(bf16[14,768,768]{2,1,0:T(8,128)(2,1)} %bitcast.353) | data formatting | bytes 33030144 | tf_op jit(solution)/shard_map/optimization_barrier | solution.py:285
  190.5 3.2 fusion.154
  194.8 3.2 fusion.12
  209.1 5.1 slice_bitcast_fusion.5
  216.4 3.0 maximum_bitcast_fusion
  226.6 2.6 multiply_reduce_fusion.1
  235.3 4.0 fusion.84
  239.3 2.9 convert_bitcast_fusion.1
  254.5 2.3 copy.150
  256.8 2.4 pad.39.clone
  259.3 3.9 reshape.330
  269.0 3.7 fusion.156
  287.5 2.4 copy.130
  292.0 2.5 constant_dynamic-update-slice_fusion.30
  314.7 3.8 fusion.41
  318.7 3.4 collective-permute-done.2
  323.0 2.7 collective-permute-done.3
  326.9 3.3 fusion.45
  330.9 193.1 %reduce-scatter.2.cloned.1.call-done = bf16[1,408,768]{2,1,0:T(8,128)(2,1)} async-done(((bf16[32,408,768]{2,1,0:T(8,128)(2,1)}), bf16[1,408,768]{2,1,0:T(8,128)(2,1)}) %reduce-scatter.2.cloned.1.call-update) | async-done | bytes 626704 | tf_op jit(solution)/shard_map/reduce_scatter | solution.py:306
  (301 shorter events, 105.5 us)
Async XLA Ops:
  7.2 193.4 %copy-start = (bf16[1,64,768]{2,1,0:T(8,128)(2,1)S(1)}, bf16[1,64,768]{2,1,0:T(8,128)(2,1)}, u32[]{:S(2)}) copy-start(bf16[1,64,768]{2,1,0:T(8,128)(2,1)} %param.12) | copy-start | bytes 294916
  7.2 141.7 %all-gather.3.cloned.1.call-start = ((), (), s32[]{:S(2)}) async-start(), calls=%async_computation.2 | async-start | bytes 20680704 | tf_op jit(solution)/shard_map/all_gather | solution.py:280
  16.5 507.5 %reduce-scatter.2.cloned.1.call-start = ((), (), s32[]{:S(2)}) async-start(), calls=%async_computation.1 | async-start | bytes 20680704 | tf_op jit(solution)/shard_map/reduce_scatter | solution.py:306
  19.7 5.5 %copy-start.4 = (bf16[1,128,768]{2,1,0:T(8,128)(2,1)S(1)}, bf16[1,128,768]{2,1,0:T(8,128)(2,1)}, u32[]{:S(2)}) copy-start(bf16[1,128,768]{2,1,0:T(8,128)(2,1)} %param.11) | copy-start | bytes 589828
  198.0 4.8 copy-start.33
  198.1 4.8 copy-start.35
  198.1 4.8 copy-start.37
  198.8 6.3 %copy-start.25 = (bf16[12,64,128]{2,1,0:T(8,128)(2,1)}, bf16[12,64,128]{2,1,0:T(8,128)(2,1)S(1)}, u32[]{:S(2)}) copy-start(bf16[12,64,128]{2,1,0:T(8,128)(2,1)S(1)} %convolution_convert_fusion.12) | copy-start | bytes 589828
  209.1 15.7 %copy-start.19 = (f32[128,768]{1,0:T(8,128)}, f32[128,768]{1,0:T(8,128)S(1)}, u32[]{:S(2)}) copy-start(f32[128,768]{1,0:T(8,128)S(1)} %get-tuple-element.94) | copy-start | bytes 1179652
  229.4 14.5 %copy-start.2 = (f32[128,768]{1,0:T(8,128)}, f32[128,768]{1,0:T(8,128)S(1)}, u32[]{:S(2)}) copy-start(f32[128,768]{1,0:T(8,128)S(1)} %multiply_add_fusion.3) | copy-start | bytes 1179652
  239.3 6.0 %copy-start.41 = (bf16[12,64,128]{2,1,0:T(8,128)(2,1)S(1)}, bf16[12,64,128]{2,1,0:T(8,128)(2,1)}, u32[]{:S(2)}) copy-start(bf16[12,64,128]{2,1,0:T(8,128)(2,1)} %copy-done.39) | copy-start | bytes 589828
  242.2 4.6 copy-start.57
  242.2 4.6 copy-start.59
  269.0 4.9 copy-start.64
  292.0 4.8 copy-start.16
  312.0 6.7 %copy-start.67 = (f32[128]{0:T(128)S(1)}, f32[128]{0:T(128)}, u32[]{:S(2)}) copy-start(f32[128]{0:T(128)} %get-tuple-element.49) | copy-start | bytes 1540
  312.0 10.1 %copy-start.3 = (f32[128,768]{1,0:T(8,128)S(1)}, f32[128,768]{1,0:T(8,128)}, u32[]{:S(2)}) copy-start(f32[128,768]{1,0:T(8,128)} %copy-done.2) | copy-start | bytes 1179652
  312.0 10.1 %copy-start.63 = (f32[128,768]{1,0:T(8,128)S(1)}, f32[128,768]{1,0:T(8,128)}, u32[]{:S(2)}) copy-start(f32[128,768]{1,0:T(8,128)} %get-tuple-element.101) | copy-start | bytes 1179652
  312.0 1.2 collective-permute-start
  313.3 13.6 %copy-start.65 = (bf16[1,64,768]{2,1,0:T(8,128)(2,1)S(1)}, bf16[1,64,768]{2,1,0:T(8,128)(2,1)}, u32[]{:S(2)}) copy-start(bf16[1,64,768]{2,1,0:T(8,128)(2,1)} %copy.124) | copy-start | bytes 294916
  313.3 5.2 collective-permute-start.1
  318.5 3.7 collective-permute-start.2
  322.1 3.7 collective-permute-start.3
  325.8 4.5 collective-permute-start.4
  (51 other events, 131.4 us)
Sparse Core Ops, SparseCore 0:
  16.6 132.1 all-gather.2
  312.1 211.8 reduce-scatter.1
